TPU v7x, 512 devices: a whole 4x4x16 slice. The times are simulated.
512 devices in a mesh: prow: 16 (over y, x), pcol: 32 (over z, core).
Axes of the slice: x: 4, y: 4, z: 16, core: 2. Of those that a mesh axis runs over, the one named last changes fastest.
Arguments:
- factor_tiles: bfloat16 [16, 1024, 1, 16, 1024], P(None, 'pcol', None, 'prow'), may hold values from -0.03125 to 0.03125
- inverse_blocks: bfloat16 [1, 16, 1024, 1024], P(None, 'prow'), may hold values from -1 to 3, as said below
- demand: bfloat16 [16, 1024, 256], P(None, 'pcol'), may hold values from -6 to 6
Outputs:
- solved: bfloat16 [1, 16, 1024, 256], P(None, 'prow')
Inputs may be any that keep to these rules, and one draw needn't show every extreme that they name: `inverse_blocks`: each [1024, 1024] block is lower triangular with a positive diagonal.
All inputs are finite; a program needn't handle non-finite values.
Results may differ from a plain program's by a relative error of at most 0.0075.
Values may be sent and summed in bfloat16 or wider, within the bound.
A program may use at most 64 MiB of HBM per device.

v0:
```python
import jax
import jax.numpy as jnp
from jax import lax
from jax.sharding import PartitionSpec as P


def on_device(factor_tiles, inverse_blocks, demand):
    block_count, slice_rows, col_slots, single, block_width = factor_tiles.shape
    columns = demand.shape[2]
    prow_size = lax.axis_size("prow")
    my_row = lax.axis_index("prow")
    row_tiles = factor_tiles.reshape(block_count, slice_rows, col_slots * block_width)
    inverse = inverse_blocks.reshape(col_slots, block_width, block_width)
    owned_blocks = jnp.zeros((col_slots, block_width, columns), jnp.bfloat16)
    pending = jnp.zeros((block_count, slice_rows, columns), jnp.float32)

    def advance(step_index, carried):
        owned_blocks, pending = carried
        owner_row = step_index % prow_size
        slot_index = step_index // prow_size
        is_owner = my_row == owner_row
        partial_sum = lax.dynamic_index_in_dim(pending, step_index, 0, keepdims=False)
        summed = lax.psum(partial_sum, "prow")
        target = lax.dynamic_index_in_dim(demand, step_index, 0, keepdims=False)
        residual = (target.astype(jnp.float32) - summed).astype(jnp.bfloat16)
        block_inv = lax.dynamic_index_in_dim(inverse, slot_index, 0, keepdims=False)
        apply_running = jnp.zeros((block_width, columns), jnp.float32)
        segment = lax.all_gather(residual, "pcol", axis=0, tiled=True)
        solved = lax.cond(
            is_owner,
            lambda: jnp.dot(block_inv, segment, preferred_element_type=jnp.float32),
            lambda: apply_running,
        ).astype(jnp.bfloat16)
        owned_blocks = jnp.where(
            is_owner,
            lax.dynamic_update_index_in_dim(owned_blocks, solved, slot_index, 0),
            owned_blocks,
        )
        pending = lax.cond(
            is_owner,
            lambda running: running
            + jnp.einsum("krw,wn->krn", row_tiles, solved, preferred_element_type=jnp.float32),
            lambda running: running,
            pending,
        )
        return (owned_blocks, pending)

    owned_blocks, pending = lax.fori_loop(0, block_count, advance, (owned_blocks, pending))
    return owned_blocks.reshape(col_slots, 1, block_width, columns)


def solution(mesh):
    placed = (
        P(None, "pcol", None, "prow", None),
        P(None, "prow", None, None),
        P(None, "pcol", None),
    )
    return jax.shard_map(
        on_device,
        mesh=mesh,
        in_specs=placed,
        out_specs=P(None, "prow", None, None),
        check_vma=False,
    )
```

profile of v0, /device:TPU:1, one launch (start us, length us, event | category | flops | bytes accessed | tf_op | source)
XLA Modules:
  0.0 1639.2 jit_solution(5200162110590774931)
XLA Ops:
  0.1 1638.4 %while.21 = (s32[]{:T(128)}, bf16[1,1024,256]{2,1,0:T(8,128)(2,1)S(1)}, f32[16,32,256]{2,1,0:T(8,128)S(1)}, s32[]{:T(128)}, bf16[16,32,256]{2,1,0:T(8,128)(2,1)}...) while((s32[]{:T(128)}, ...), condition=%wide.region_6.7_spmd.clone, body=%wide.region_0.6_spmd.clone.sunk | while | flops 806256640 | bytes 13320484 | solution.py:48
  0.1 61.6 %psum.16 = f32[32,256]{1,0:T(8,128)S(1)} all-reduce(f32[32,256]{1,0:T(8,128)S(1)} %dynamic-slice_bitcast_fusion.2), channel_id=1, replica_groups=mesh['prow'=16,'pcol'=32] {'prow'}, use_global_device_ids=true, to_apply=%region_1.1 | all-reduce | flops 8192 | bytes 65536 | tf_op jit(solution)/shard_map/while/body/eval_jaxpr/psum | solution.py:23
  62.4 52.0 %all_gather.12 = bf16[1024,256]{1,0:T(8,128)(2,1)S(1)} all-gather(bf16[32,256]{1,0:T(8,128)(2,1)S(1)} %fusion.10), channel_id=1, replica_groups=mesh['prow'=16,'pcol'=32] {'pcol'}, dimensions={0}, use_global_device_ids=true | all-gather | bytes 540672 | tf_op jit(solution)/shard_map/while/body/eval_jaxpr/all_gather | solution.py:28
  120.4 55.8 %psum.16 = f32[32,256]{1,0:T(8,128)S(1)} all-reduce(f32[32,256]{1,0:T(8,128)S(1)} %dynamic-slice_bitcast_fusion.2), channel_id=1, replica_groups=mesh['prow'=16,'pcol'=32] {'prow'}, use_global_device_ids=true, to_apply=%region_1.1 | all-reduce | flops 8192 | bytes 65536 | tf_op jit(solution)/shard_map/while/body/eval_jaxpr/psum | solution.py:23
  220.5 58.3 %psum.16 = f32[32,256]{1,0:T(8,128)S(1)} all-reduce(f32[32,256]{1,0:T(8,128)S(1)} %dynamic-slice_bitcast_fusion.2), channel_id=1, replica_groups=mesh['prow'=16,'pcol'=32] {'prow'}, use_global_device_ids=true, to_apply=%region_1.1 | all-reduce | flops 8192 | bytes 65536 | tf_op jit(solution)/shard_map/while/body/eval_jaxpr/psum | solution.py:23
  279.5 44.1 %all_gather.12 = bf16[1024,256]{1,0:T(8,128)(2,1)S(1)} all-gather(bf16[32,256]{1,0:T(8,128)(2,1)S(1)} %fusion.10), channel_id=1, replica_groups=mesh['prow'=16,'pcol'=32] {'pcol'}, dimensions={0}, use_global_device_ids=true | all-gather | bytes 540672 | tf_op jit(solution)/shard_map/while/body/eval_jaxpr/all_gather | solution.py:28
  325.3 55.8 %psum.16 = f32[32,256]{1,0:T(8,128)S(1)} all-reduce(f32[32,256]{1,0:T(8,128)S(1)} %dynamic-slice_bitcast_fusion.2), channel_id=1, replica_groups=mesh['prow'=16,'pcol'=32] {'prow'}, use_global_device_ids=true, to_apply=%region_1.1 | all-reduce | flops 8192 | bytes 65536 | tf_op jit(solution)/shard_map/while/body/eval_jaxpr/psum | solution.py:23
  425.4 55.8 %psum.16 = f32[32,256]{1,0:T(8,128)S(1)} all-reduce(f32[32,256]{1,0:T(8,128)S(1)} %dynamic-slice_bitcast_fusion.2), channel_id=1, replica_groups=mesh['prow'=16,'pcol'=32] {'prow'}, use_global_device_ids=true, to_apply=%region_1.1 | all-reduce | flops 8192 | bytes 65536 | tf_op jit(solution)/shard_map/while/body/eval_jaxpr/psum | solution.py:23
  481.9 43.9 %all_gather.12 = bf16[1024,256]{1,0:T(8,128)(2,1)S(1)} all-gather(bf16[32,256]{1,0:T(8,128)(2,1)S(1)} %fusion.10), channel_id=1, replica_groups=mesh['prow'=16,'pcol'=32] {'pcol'}, dimensions={0}, use_global_device_ids=true | all-gather | bytes 540672 | tf_op jit(solution)/shard_map/while/body/eval_jaxpr/all_gather | solution.py:28
  527.5 55.8 %psum.16 = f32[32,256]{1,0:T(8,128)S(1)} all-reduce(f32[32,256]{1,0:T(8,128)S(1)} %dynamic-slice_bitcast_fusion.2), channel_id=1, replica_groups=mesh['prow'=16,'pcol'=32] {'prow'}, use_global_device_ids=true, to_apply=%region_1.1 | all-reduce | flops 8192 | bytes 65536 | tf_op jit(solution)/shard_map/while/body/eval_jaxpr/psum | solution.py:23
  627.6 55.8 %psum.16 = f32[32,256]{1,0:T(8,128)S(1)} all-reduce(f32[32,256]{1,0:T(8,128)S(1)} %dynamic-slice_bitcast_fusion.2), channel_id=1, replica_groups=mesh['prow'=16,'pcol'=32] {'prow'}, use_global_device_ids=true, to_apply=%region_1.1 | all-reduce | flops 8192 | bytes 65536 | tf_op jit(solution)/shard_map/while/body/eval_jaxpr/psum | solution.py:23
  684.1 43.9 %all_gather.12 = bf16[1024,256]{1,0:T(8,128)(2,1)S(1)} all-gather(bf16[32,256]{1,0:T(8,128)(2,1)S(1)} %fusion.10), channel_id=1, replica_groups=mesh['prow'=16,'pcol'=32] {'pcol'}, dimensions={0}, use_global_device_ids=true | all-gather | bytes 540672 | tf_op jit(solution)/shard_map/while/body/eval_jaxpr/all_gather | solution.py:28
  729.7 55.8 %psum.16 = f32[32,256]{1,0:T(8,128)S(1)} all-reduce(f32[32,256]{1,0:T(8,128)S(1)} %dynamic-slice_bitcast_fusion.2), channel_id=1, replica_groups=mesh['prow'=16,'pcol'=32] {'prow'}, use_global_device_ids=true, to_apply=%region_1.1 | all-reduce | flops 8192 | bytes 65536 | tf_op jit(solution)/shard_map/while/body/eval_jaxpr/psum | solution.py:23
  829.8 55.8 %psum.16 = f32[32,256]{1,0:T(8,128)S(1)} all-reduce(f32[32,256]{1,0:T(8,128)S(1)} %dynamic-slice_bitcast_fusion.2), channel_id=1, replica_groups=mesh['prow'=16,'pcol'=32] {'prow'}, use_global_device_ids=true, to_apply=%region_1.1 | all-reduce | flops 8192 | bytes 65536 | tf_op jit(solution)/shard_map/while/body/eval_jaxpr/psum | solution.py:23
  886.3 43.9 %all_gather.12 = bf16[1024,256]{1,0:T(8,128)(2,1)S(1)} all-gather(bf16[32,256]{1,0:T(8,128)(2,1)S(1)} %fusion.10), channel_id=1, replica_groups=mesh['prow'=16,'pcol'=32] {'pcol'}, dimensions={0}, use_global_device_ids=true | all-gather | bytes 540672 | tf_op jit(solution)/shard_map/while/body/eval_jaxpr/all_gather | solution.py:28
  931.8 55.8 %psum.16 = f32[32,256]{1,0:T(8,128)S(1)} all-reduce(f32[32,256]{1,0:T(8,128)S(1)} %dynamic-slice_bitcast_fusion.2), channel_id=1, replica_groups=mesh['prow'=16,'pcol'=32] {'prow'}, use_global_device_ids=true, to_apply=%region_1.1 | all-reduce | flops 8192 | bytes 65536 | tf_op jit(solution)/shard_map/while/body/eval_jaxpr/psum | solution.py:23
  1031.9 55.8 %psum.16 = f32[32,256]{1,0:T(8,128)S(1)} all-reduce(f32[32,256]{1,0:T(8,128)S(1)} %dynamic-slice_bitcast_fusion.2), channel_id=1, replica_groups=mesh['prow'=16,'pcol'=32] {'prow'}, use_global_device_ids=true, to_apply=%region_1.1 | all-reduce | flops 8192 | bytes 65536 | tf_op jit(solution)/shard_map/while/body/eval_jaxpr/psum | solution.py:23
  1088.4 43.9 %all_gather.12 = bf16[1024,256]{1,0:T(8,128)(2,1)S(1)} all-gather(bf16[32,256]{1,0:T(8,128)(2,1)S(1)} %fusion.10), channel_id=1, replica_groups=mesh['prow'=16,'pcol'=32] {'pcol'}, dimensions={0}, use_global_device_ids=true | all-gather | bytes 540672 | tf_op jit(solution)/shard_map/while/body/eval_jaxpr/all_gather | solution.py:28
  1134.0 55.8 %psum.16 = f32[32,256]{1,0:T(8,128)S(1)} all-reduce(f32[32,256]{1,0:T(8,128)S(1)} %dynamic-slice_bitcast_fusion.2), channel_id=1, replica_groups=mesh['prow'=16,'pcol'=32] {'prow'}, use_global_device_ids=true, to_apply=%region_1.1 | all-reduce | flops 8192 | bytes 65536 | tf_op jit(solution)/shard_map/while/body/eval_jaxpr/psum | solution.py:23
  1234.1 55.8 %psum.16 = f32[32,256]{1,0:T(8,128)S(1)} all-reduce(f32[32,256]{1,0:T(8,128)S(1)} %dynamic-slice_bitcast_fusion.2), channel_id=1, replica_groups=mesh['prow'=16,'pcol'=32] {'prow'}, use_global_device_ids=true, to_apply=%region_1.1 | all-reduce | flops 8192 | bytes 65536 | tf_op jit(solution)/shard_map/while/body/eval_jaxpr/psum | solution.py:23
  1290.6 43.9 %all_gather.12 = bf16[1024,256]{1,0:T(8,128)(2,1)S(1)} all-gather(bf16[32,256]{1,0:T(8,128)(2,1)S(1)} %fusion.10), channel_id=1, replica_groups=mesh['prow'=16,'pcol'=32] {'pcol'}, dimensions={0}, use_global_device_ids=true | all-gather | bytes 540672 | tf_op jit(solution)/shard_map/while/body/eval_jaxpr/all_gather | solution.py:28
  1336.2 55.8 %psum.16 = f32[32,256]{1,0:T(8,128)S(1)} all-reduce(f32[32,256]{1,0:T(8,128)S(1)} %dynamic-slice_bitcast_fusion.2), channel_id=1, replica_groups=mesh['prow'=16,'pcol'=32] {'prow'}, use_global_device_ids=true, to_apply=%region_1.1 | all-reduce | flops 8192 | bytes 65536 | tf_op jit(solution)/shard_map/while/body/eval_jaxpr/psum | solution.py:23
  1436.3 55.8 %psum.16 = f32[32,256]{1,0:T(8,128)S(1)} all-reduce(f32[32,256]{1,0:T(8,128)S(1)} %dynamic-slice_bitcast_fusion.2), channel_id=1, replica_groups=mesh['prow'=16,'pcol'=32] {'prow'}, use_global_device_ids=true, to_apply=%region_1.1 | all-reduce | flops 8192 | bytes 65536 | tf_op jit(solution)/shard_map/while/body/eval_jaxpr/psum | solution.py:23
  1538.4 55.8 %psum.16 = f32[32,256]{1,0:T(8,128)S(1)} all-reduce(f32[32,256]{1,0:T(8,128)S(1)} %dynamic-slice_bitcast_fusion.2), channel_id=1, replica_groups=mesh['prow'=16,'pcol'=32] {'prow'}, use_global_device_ids=true, to_apply=%region_1.1 | all-reduce | flops 8192 | bytes 65536 | tf_op jit(solution)/shard_map/while/body/eval_jaxpr/psum | solution.py:23
  (158 shorter events, 441.0 us)
Async XLA Ops:
  114.4 4.2 copy-start
  218.8 1.4 copy-start
  323.6 1.4 copy-start
  423.8 1.4 copy-start
  525.8 1.4 copy-start
  625.9 1.4 copy-start
  728.0 1.4 copy-start
  828.1 1.4 copy-start
  930.2 1.4 copy-start
  1030.3 1.4 copy-start
  1132.3 1.4 copy-start
  1232.5 1.4 copy-start
  1334.5 1.4 copy-start
  1434.6 1.4 copy-start
  1536.7 1.4 copy-start
  1636.8 1.4 copy-start
  1638.4 0.8 copy-start.1
where the time goes:
time: 1640 us
  blocking collectives  1600 us (98%)
  local copies, waits for them, and re-layouts  23 us (1%)
    psum x16, blocking collectives, advance(): summed = lax.psum(partial_sum, 'prow')  901 us
    all_gather x16, blocking collectives, advance(): segment = lax.all_gather(residual, 'pcol', axis=0, tiled=True)  695 us

commit v1 on v0

--- a/solution.py
+++ b/solution.py
@@ -20,7 +20,7 @@
         slot_index = step_index // prow_size
         is_owner = my_row == owner_row
         partial_sum = lax.dynamic_index_in_dim(pending, step_index, 0, keepdims=False)
-        summed = lax.psum(partial_sum, "prow")
+        summed = jnp.sum(lax.all_gather(partial_sum, "prow"), axis=0)
         target = lax.dynamic_index_in_dim(demand, step_index, 0, keepdims=False)
         residual = (target.astype(jnp.float32) - summed).astype(jnp.bfloat16)
         block_inv = lax.dynamic_index_in_dim(inverse, slot_index, 0, keepdims=False)

time: 1640 us -> 931 us (0.57)
  blocking collectives: 1600 us -> 883 us
    psum x16 -> x0, blocking collectives: 901 us -> none  [advance(): summed = lax.psum(partial_sum, 'prow')]
    all_gather x0 -> x16, blocking collectives: none -> 328 us  [advance(): summed = jnp.sum(lax.all_gather(partial_sum, 'prow'), axis=0)]
    all_gather x16, blocking collectives: 695 us -> 555 us  [advance(): segment = lax.all_gather(residual, 'pcol', axis=0, tiled=True)]
where the time goes in v1:
time: 931 us; the launch traced here: 928 us
  blocking collectives  883 us (95%)
  local copies, waits for them, and re-layouts  23 us (2%)
  other arithmetic  15.5 us (2%)
    all_gather x16, blocking collectives, advance(): segment = lax.all_gather(residual, 'pcol', axis=0, tiled=True)  555 us
    all_gather x16, blocking collectives, advance(): summed = jnp.sum(lax.all_gather(partial_sum, 'prow'), axis=0)  328 us

profile of v1, /device:TPU:1, one launch (start us, length us, event | category | flops | bytes accessed | tf_op | source)
XLA Modules:
  0.0 927.6 jit_solution(16236992343223026364)
XLA Ops:
  0.1 926.7 %while.21 = (s32[]{:T(128)}, bf16[1,1024,256]{2,1,0:T(8,128)(2,1)S(1)}, f32[16,32,256]{2,1,0:T(8,128)S(1)}, s32[]{:T(128)}, bf16[16,32,256]{2,1,0:T(8,128)(2,1)}...) while((s32[]{:T(128)}, ...), condition=%wide.region_6.7_spmd.clone, body=%wide.region_0.6_spmd.clone.sunk | while | flops 806371328 | bytes 14369072 | solution.py:48
  20.8 43.3 %all_gather.26 = bf16[1024,256]{1,0:T(8,128)(2,1)S(1)} all-gather(bf16[32,256]{1,0:T(8,128)(2,1)S(1)} %fusion.10), channel_id=1, replica_groups=mesh['prow'=16,'pcol'=32] {'pcol'}, dimensions={0}, use_global_device_ids=true | all-gather | bytes 540672 | tf_op jit(solution)/shard_map/while/body/eval_jaxpr/all_gather | solution.py:28
  86.6 33.6 %all_gather.26 = bf16[1024,256]{1,0:T(8,128)(2,1)S(1)} all-gather(bf16[32,256]{1,0:T(8,128)(2,1)S(1)} %fusion.10), channel_id=1, replica_groups=mesh['prow'=16,'pcol'=32] {'pcol'}, dimensions={0}, use_global_device_ids=true | all-gather | bytes 540672 | tf_op jit(solution)/shard_map/while/body/eval_jaxpr/all_gather | solution.py:28
  121.8 22.1 %all_gather.25 = f32[16,32,256]{2,1,0:T(8,128)S(1)} all-gather(f32[1,32,256]{2,1,0:T(8,128)S(1)} %constant_dynamic-slice_fusion.2), channel_id=1, replica_groups=mesh['prow'=16,'pcol'=32] {'prow'}, dimensions={0}, use_global_device_ids=true | all-gather | bytes 557056 | tf_op jit(solution)/shard_map/while/body/eval_jaxpr/all_gather | solution.py:23
  144.7 35.0 %all_gather.26 = bf16[1024,256]{1,0:T(8,128)(2,1)S(1)} all-gather(bf16[32,256]{1,0:T(8,128)(2,1)S(1)} %fusion.10), channel_id=1, replica_groups=mesh['prow'=16,'pcol'=32] {'pcol'}, dimensions={0}, use_global_device_ids=true | all-gather | bytes 540672 | tf_op jit(solution)/shard_map/while/body/eval_jaxpr/all_gather | solution.py:28
  201.9 33.3 %all_gather.26 = bf16[1024,256]{1,0:T(8,128)(2,1)S(1)} all-gather(bf16[32,256]{1,0:T(8,128)(2,1)S(1)} %fusion.10), channel_id=1, replica_groups=mesh['prow'=16,'pcol'=32] {'pcol'}, dimensions={0}, use_global_device_ids=true | all-gather | bytes 540672 | tf_op jit(solution)/shard_map/while/body/eval_jaxpr/all_gather | solution.py:28
  236.9 23.2 %all_gather.25 = f32[16,32,256]{2,1,0:T(8,128)S(1)} all-gather(f32[1,32,256]{2,1,0:T(8,128)S(1)} %constant_dynamic-slice_fusion.2), channel_id=1, replica_groups=mesh['prow'=16,'pcol'=32] {'prow'}, dimensions={0}, use_global_device_ids=true | all-gather | bytes 557056 | tf_op jit(solution)/shard_map/while/body/eval_jaxpr/all_gather | solution.py:23
  260.9 35.1 %all_gather.26 = bf16[1024,256]{1,0:T(8,128)(2,1)S(1)} all-gather(bf16[32,256]{1,0:T(8,128)(2,1)S(1)} %fusion.10), channel_id=1, replica_groups=mesh['prow'=16,'pcol'=32] {'pcol'}, dimensions={0}, use_global_device_ids=true | all-gather | bytes 540672 | tf_op jit(solution)/shard_map/while/body/eval_jaxpr/all_gather | solution.py:28
  317.8 33.1 %all_gather.26 = bf16[1024,256]{1,0:T(8,128)(2,1)S(1)} all-gather(bf16[32,256]{1,0:T(8,128)(2,1)S(1)} %fusion.10), channel_id=1, replica_groups=mesh['prow'=16,'pcol'=32] {'pcol'}, dimensions={0}, use_global_device_ids=true | all-gather | bytes 540672 | tf_op jit(solution)/shard_map/while/body/eval_jaxpr/all_gather | solution.py:28
  372.4 35.3 %all_gather.26 = bf16[1024,256]{1,0:T(8,128)(2,1)S(1)} all-gather(bf16[32,256]{1,0:T(8,128)(2,1)S(1)} %fusion.10), channel_id=1, replica_groups=mesh['prow'=16,'pcol'=32] {'pcol'}, dimensions={0}, use_global_device_ids=true | all-gather | bytes 540672 | tf_op jit(solution)/shard_map/while/body/eval_jaxpr/all_gather | solution.py:28
  409.4 22.1 %all_gather.25 = f32[16,32,256]{2,1,0:T(8,128)S(1)} all-gather(f32[1,32,256]{2,1,0:T(8,128)S(1)} %constant_dynamic-slice_fusion.2), channel_id=1, replica_groups=mesh['prow'=16,'pcol'=32] {'prow'}, dimensions={0}, use_global_device_ids=true | all-gather | bytes 557056 | tf_op jit(solution)/shard_map/while/body/eval_jaxpr/all_gather | solution.py:23
  432.3 33.1 %all_gather.26 = bf16[1024,256]{1,0:T(8,128)(2,1)S(1)} all-gather(bf16[32,256]{1,0:T(8,128)(2,1)S(1)} %fusion.10), channel_id=1, replica_groups=mesh['prow'=16,'pcol'=32] {'pcol'}, dimensions={0}, use_global_device_ids=true | all-gather | bytes 540672 | tf_op jit(solution)/shard_map/while/body/eval_jaxpr/all_gather | solution.py:28
  488.1 35.3 %all_gather.26 = bf16[1024,256]{1,0:T(8,128)(2,1)S(1)} all-gather(bf16[32,256]{1,0:T(8,128)(2,1)S(1)} %fusion.10), channel_id=1, replica_groups=mesh['prow'=16,'pcol'=32] {'pcol'}, dimensions={0}, use_global_device_ids=true | all-gather | bytes 540672 | tf_op jit(solution)/shard_map/while/body/eval_jaxpr/all_gather | solution.py:28
  545.5 33.3 %all_gather.26 = bf16[1024,256]{1,0:T(8,128)(2,1)S(1)} all-gather(bf16[32,256]{1,0:T(8,128)(2,1)S(1)} %fusion.10), channel_id=1, replica_groups=mesh['prow'=16,'pcol'=32] {'pcol'}, dimensions={0}, use_global_device_ids=true | all-gather | bytes 540672 | tf_op jit(solution)/shard_map/while/body/eval_jaxpr/all_gather | solution.py:28
  580.5 22.1 %all_gather.25 = f32[16,32,256]{2,1,0:T(8,128)S(1)} all-gather(f32[1,32,256]{2,1,0:T(8,128)S(1)} %constant_dynamic-slice_fusion.2), channel_id=1, replica_groups=mesh['prow'=16,'pcol'=32] {'prow'}, dimensions={0}, use_global_device_ids=true | all-gather | bytes 557056 | tf_op jit(solution)/shard_map/while/body/eval_jaxpr/all_gather | solution.py:23
  603.4 35.0 %all_gather.26 = bf16[1024,256]{1,0:T(8,128)(2,1)S(1)} all-gather(bf16[32,256]{1,0:T(8,128)(2,1)S(1)} %fusion.10), channel_id=1, replica_groups=mesh['prow'=16,'pcol'=32] {'pcol'}, dimensions={0}, use_global_device_ids=true | all-gather | bytes 540672 | tf_op jit(solution)/shard_map/while/body/eval_jaxpr/all_gather | solution.py:28
  659.9 33.3 %all_gather.26 = bf16[1024,256]{1,0:T(8,128)(2,1)S(1)} all-gather(bf16[32,256]{1,0:T(8,128)(2,1)S(1)} %fusion.10), channel_id=1, replica_groups=mesh['prow'=16,'pcol'=32] {'pcol'}, dimensions={0}, use_global_device_ids=true | all-gather | bytes 540672 | tf_op jit(solution)/shard_map/while/body/eval_jaxpr/all_gather | solution.py:28
  694.9 23.3 %all_gather.25 = f32[16,32,256]{2,1,0:T(8,128)S(1)} all-gather(f32[1,32,256]{2,1,0:T(8,128)S(1)} %constant_dynamic-slice_fusion.2), channel_id=1, replica_groups=mesh['prow'=16,'pcol'=32] {'prow'}, dimensions={0}, use_global_device_ids=true | all-gather | bytes 557056 | tf_op jit(solution)/shard_map/while/body/eval_jaxpr/all_gather | solution.py:23
  719.0 35.0 %all_gather.26 = bf16[1024,256]{1,0:T(8,128)(2,1)S(1)} all-gather(bf16[32,256]{1,0:T(8,128)(2,1)S(1)} %fusion.10), channel_id=1, replica_groups=mesh['prow'=16,'pcol'=32] {'pcol'}, dimensions={0}, use_global_device_ids=true | all-gather | bytes 540672 | tf_op jit(solution)/shard_map/while/body/eval_jaxpr/all_gather | solution.py:28
  755.7 20.5 %all_gather.25 = f32[16,32,256]{2,1,0:T(8,128)S(1)} all-gather(f32[1,32,256]{2,1,0:T(8,128)S(1)} %constant_dynamic-slice_fusion.2), channel_id=1, replica_groups=mesh['prow'=16,'pcol'=32] {'prow'}, dimensions={0}, use_global_device_ids=true | all-gather | bytes 557056 | tf_op jit(solution)/shard_map/while/body/eval_jaxpr/all_gather | solution.py:23
  776.9 33.2 %all_gather.26 = bf16[1024,256]{1,0:T(8,128)(2,1)S(1)} all-gather(bf16[32,256]{1,0:T(8,128)(2,1)S(1)} %fusion.10), channel_id=1, replica_groups=mesh['prow'=16,'pcol'=32] {'pcol'}, dimensions={0}, use_global_device_ids=true | all-gather | bytes 540672 | tf_op jit(solution)/shard_map/while/body/eval_jaxpr/all_gather | solution.py:28
  831.6 35.3 %all_gather.26 = bf16[1024,256]{1,0:T(8,128)(2,1)S(1)} all-gather(bf16[32,256]{1,0:T(8,128)(2,1)S(1)} %fusion.10), channel_id=1, replica_groups=mesh['prow'=16,'pcol'=32] {'pcol'}, dimensions={0}, use_global_device_ids=true | all-gather | bytes 540672 | tf_op jit(solution)/shard_map/while/body/eval_jaxpr/all_gather | solution.py:28
  868.6 22.7 %all_gather.25 = f32[16,32,256]{2,1,0:T(8,128)S(1)} all-gather(f32[1,32,256]{2,1,0:T(8,128)S(1)} %constant_dynamic-slice_fusion.2), channel_id=1, replica_groups=mesh['prow'=16,'pcol'=32] {'prow'}, dimensions={0}, use_global_device_ids=true | all-gather | bytes 557056 | tf_op jit(solution)/shard_map/while/body/eval_jaxpr/all_gather | solution.py:23
  892.1 33.1 %all_gather.26 = bf16[1024,256]{1,0:T(8,128)(2,1)S(1)} all-gather(bf16[32,256]{1,0:T(8,128)(2,1)S(1)} %fusion.10), channel_id=1, replica_groups=mesh['prow'=16,'pcol'=32] {'pcol'}, dimensions={0}, use_global_device_ids=true | all-gather | bytes 540672 | tf_op jit(solution)/shard_map/while/body/eval_jaxpr/all_gather | solution.py:28
  (174 shorter events, 234.0 us)
Async XLA Ops:
  64.1 4.2 copy-start
  120.2 1.4 copy-start
  179.8 1.4 copy-start
  235.2 1.4 copy-start
  296.0 1.4 copy-start
  350.9 1.4 copy-start
  407.7 1.4 copy-start
  465.3 1.4 copy-start
  523.3 1.4 copy-start
  578.8 1.4 copy-start
  638.4 1.4 copy-start
  693.2 1.4 copy-start
  754.0 1.4 copy-start
  810.1 1.4 copy-start
  866.9 1.4 copy-start
  925.2 1.4 copy-start
  926.8 0.8 copy-start.1
